TPU v7x, 768 devices: a whole 4x8x12 slice. The times are simulated.
768 devices in a mesh: lst: 32 (over y, x), freq: 24 (over z, core).
Axes of the slice: x: 4, y: 8, z: 12, core: 2. Of those that a mesh axis runs over, the one named last changes fastest.
Arguments:
- visibilities: bfloat16 [2, 768, 288, 768], P(None, ('lst', 'freq')), may hold values from -6 to 6
- model_vis: bfloat16 [2, 768, 288, 768], P(None, ('lst', 'freq')), may hold values from -6 to 6
- antenna_gains: bfloat16 [2, 768, 256, 768], P(None, ('lst', 'freq')), may hold values from -6 to 6
- baseline_antenna_index: int32 [2, 288], replicated, may hold values from 0 to 255, as said below
- flag_tiles: int32 [768, 288, 6], P(('lst', 'freq')), may hold values 0 or 1
- kernel: float32 [5], replicated, may hold values from 0.1 to 0.3
Outputs:
- smoothed_step: bfloat16 [2, 768, 256, 768], P(None, 'lst', None, 'freq')
Inputs may be any that keep to these rules, and one draw needn't show every extreme that they name: `baseline_antenna_index`: in each column the two antennas differ; every antenna appears in the first row.
All inputs are finite; a program needn't handle non-finite values. No bound on the sum of `flag_tiles` on one device may be relied on, other than what follows from the above.
Results may differ from a plain program's by a relative error of at most 0.0053.
Values may be sent and summed in bfloat16 or wider, within the bound.
A program may use at most 32 MiB of HBM per device.

v0:
```python
import jax
import jax.numpy as jnp
from jax import lax
from jax.sharding import PartitionSpec as P


def extended(array, sides, width):
    for axis, dim in sides:
        size, length = (lax.axis_size(axis), array.shape[dim])
        up = [(i, (i + 1) % size) for i in range(size)]
        down = [(j, i) for i, j in up]
        last = lax.slice_in_dim(array, length - width, length, axis=dim)
        leading = lax.slice_in_dim(array, 0, width, axis=dim)
        before = lax.ppermute(last, axis, up)
        after = lax.ppermute(leading, axis, down)
        array = jnp.concatenate([before, array, after], axis=dim)
    return array


def baseline_terms(leading_gain, trailing_gain, data_row, model_row, weight):
    first_re, first_im = (leading_gain[0], leading_gain[1])
    second_re, second_im = (trailing_gain[0], trailing_gain[1])
    data_re, data_im = (data_row[0], data_row[1])
    model_re, model_im = (model_row[0], model_row[1])
    cross_re = first_re * second_re + first_im * second_im
    cross_im = first_im * second_re - first_re * second_im
    pred_re = cross_re * model_re - cross_im * model_im
    pred_im = cross_re * model_im + cross_im * model_re
    resid_re = weight * (data_re - pred_re)
    resid_im = weight * (data_im - pred_im)
    along_re = second_re * model_re + second_im * model_im
    along_im = second_im * model_re - second_re * model_im
    leading_term = jnp.stack(
        [resid_re * along_re - resid_im * along_im, resid_re * along_im + resid_im * along_re]
    )
    other_re = first_re * model_re - first_im * model_im
    other_im = first_re * model_im + first_im * model_re
    trailing_term = jnp.stack(
        [resid_re * other_re + resid_im * other_im, resid_re * other_im - resid_im * other_re]
    )
    return (leading_term, trailing_term)


def body(visibilities, model_vis, antenna_gains, baseline_antenna_index, flag_tiles, kernel):
    antenna_list = antenna_gains.shape[2]
    baseline_list = baseline_antenna_index.shape[1]
    tile_width = visibilities.shape[3] // flag_tiles.shape[2]
    segment_labels = lax.broadcasted_iota(jnp.int32, (baseline_list, antenna_list), 1)
    hot_first = (baseline_antenna_index[0][:, None] == segment_labels).astype(jnp.bfloat16)
    hot_second = (baseline_antenna_index[1][:, None] == segment_labels).astype(jnp.bfloat16)
    leading_gain = jnp.einsum(
        "ba,rtac->rtbc", hot_first, antenna_gains, preferred_element_type=jnp.float32
    )
    trailing_gain = jnp.einsum(
        "ba,rtac->rtbc", hot_second, antenna_gains, preferred_element_type=jnp.float32
    )
    weight = jnp.repeat(flag_tiles.astype(jnp.float32), tile_width, axis=2)
    leading_term, trailing_term = baseline_terms(
        leading_gain,
        trailing_gain,
        visibilities.astype(jnp.float32),
        model_vis.astype(jnp.float32),
        weight,
    )
    antenna_sums = jnp.einsum(
        "ba,rtbc->rtac",
        hot_first,
        leading_term.astype(jnp.bfloat16),
        preferred_element_type=jnp.float32,
    )
    antenna_sums = antenna_sums + jnp.einsum(
        "ba,rtbc->rtac",
        hot_second,
        trailing_term.astype(jnp.bfloat16),
        preferred_element_type=jnp.float32,
    )
    baseline_counts = jnp.einsum(
        "ba,tbk->tak",
        hot_first + hot_second,
        flag_tiles.astype(jnp.bfloat16),
        preferred_element_type=jnp.float32,
    )
    partial_value = (
        antenna_sums / (1.0 + jnp.repeat(baseline_counts, tile_width, axis=2))[None]
    ).astype(jnp.bfloat16)
    half_width = (kernel.shape[0] - 1) // 2
    beside = extended(partial_value, (("lst", 1),), 1)
    position = lax.axis_index("freq")
    groups = lax.axis_size("freq")
    borrowed = jnp.where(
        position >= groups - half_width,
        beside[:, 0:1],
        jnp.where(position < half_width, beside[:, 2:3], jnp.zeros_like(partial_value)),
    )
    received = lax.all_to_all(
        jnp.stack([partial_value, borrowed]), "freq", split_axis=4, concat_axis=2, tiled=True
    )
    padded = jnp.concatenate(
        [received[1][:, groups - half_width :], received[0], received[1][:, :half_width]], axis=1
    )
    row_count = padded.shape[1] - 2 * half_width
    update = jnp.zeros((padded.shape[0], row_count, padded.shape[2], padded.shape[3]), jnp.float32)
    for shift_index in range(2 * half_width + 1):
        update = update + kernel[shift_index] * padded[
            :, shift_index : shift_index + row_count
        ].astype(jnp.float32)
    return update.astype(jnp.bfloat16)


def solution(mesh):
    in_specs = (
        P(None, ("lst", "freq"), None, None),
        P(None, ("lst", "freq"), None, None),
        P(None, ("lst", "freq"), None, None),
        P(),
        P(("lst", "freq"), None, None),
        P(),
    )
    out_specs = P(None, "lst", None, "freq")
    return jax.shard_map(body, mesh=mesh, in_specs=in_specs, out_specs=out_specs, check_vma=False)
```

profile of v0, /device:TPU:30, one launch (start us, length us, event | category | flops | bytes accessed | tf_op | source)
XLA Modules:
  0.0 122.9 jit_solution(5497857719608955013)
XLA Ops:
  0.0 0.0 copy-start
  0.0 0.8 slice_reduce_fusion.1
  0.8 0.4 copy-done
  1.2 1.7 %fusion.20 = f32[288,2,768]{2,0,1:T(8,128)} fusion(bf16[2,1,256,768]{3,2,1,0:T(8,128)(2,1)S(1)} %copy-done, s32[288]{0:T(512)S(1)} %get-tuple-element.5), kind=kOutput, calls=%fused_computation.47 | convolution fusion | flops 226566144 | bytes 2557056 | tf_op jit(solution)/shard_map/ba,rtac->rtbc/dot_general | solution.py:51
  2.8 0.0 copy-start.4
  2.8 0.4 convolution_bitcast_fusion
  3.3 0.3 copy-done.4
  3.5 0.1 copy.41
  3.7 1.4 %broadcast_in_dim.12 = f32[288,6,128]{2,1,0:T(8,128)} broadcast(f32[288,6]{1,0:T(8,128)S(1)} %bitcast.110), dimensions={0,1} | broadcast | bytes 891648 | tf_op jit(solution)/shard_map/broadcast_in_dim | solution.py:57
  5.1 1.5 %broadcast_in_dim.13 = f32[1,1,288,768]{3,2,1,0:T(8,128)S(1)} reshape(f32[288,6,128]{2,1,0:T(8,128)} %broadcast_in_dim.12) | data formatting | bytes 1769472 | tf_op jit(solution)/shard_map/broadcast_in_dim | solution.py:57
  6.6 0.0 copy-start.2
  6.6 1.4 %convert_element_type.52 = f32[2,1,288,768]{3,2,1,0:T(8,128)S(1)} convert(bf16[2,1,288,768]{3,2,1,0:T(8,128)(2,1)} %param.7) | non-fusion elementwise | flops 442368 | bytes 2654208 | tf_op jit(solution)/shard_map/convert_element_type | solution.py:62
  7.9 0.0 copy-done.2
  8.0 0.0 copy-start.1
  8.0 0.1 convert_element_type.51
  8.1 0.3 convolution_add_fusion
  8.4 1.1 copy-done.1
  9.5 0.2 fusion.14
  9.7 0.7 fusion.24
  10.4 0.5 fusion.22
  10.9 0.2 fusion.25
  11.2 0.2 fusion.23
  11.4 0.7 fusion.3
  12.1 0.1 broadcast_in_dim.14
  12.2 0.7 fusion
  12.9 4.6 %collective-permute-start = (bf16[2,1,256,768]{2,3,0,1:T(8,128)(2,1)S(1)}, bf16[2,1,256,768]{2,3,0,1:T(8,128)(2,1)S(1)}, u32[]{:S(2)}, u32[]{:S(2)}) collective-permute-start(bf16[2,1,256,768]{2,3,0,1:T(8,128)(2,1)S(1)} %fusion), channel_id=1, source_target_pairs={{0,24},{24,48},{48,72},{72,96},{96,120},{120,144},{144,168},{168,1... | collective-permute-start | bytes 2359304 | tf_op jit(solution)/shard_map/ppermute | solution.py:14
  17.5 1.9 %collective-permute-start.1 = (bf16[2,1,256,768]{2,3,0,1:T(8,128)(2,1)S(1)}, bf16[2,1,256,768]{2,3,0,1:T(8,128)(2,1)S(1)}, u32[]{:S(2)}, u32[]{:S(2)}) collective-permute-start(bf16[2,1,256,768]{2,3,0,1:T(8,128)(2,1)S(1)} %fusion), channel_id=1, source_target_pairs={{24,0},{48,24},{72,48},{96,72},{120,96},{144,120},{168,144},{192,1... | collective-permute-start | bytes 2359304 | tf_op jit(solution)/shard_map/ppermute | solution.py:15
  19.4 14.8 %collective-permute-done = bf16[2,1,256,768]{2,3,0,1:T(8,128)(2,1)S(1)} collective-permute-done((bf16[2,1,256,768]{2,3,0,1:T(8,128)(2,1)S(1)}, bf16[2,1,256,768]{2,3,0,1:T(8,128)(2,1)S(1)}, u32[]{:S(2)}, u32[]{:S(2)}) %collective-permute-start) | collective-permute-done | bytes 786464 | tf_op jit(solution)/shard_map/ppermute | solution.py:14
  34.3 7.4 %collective-permute-done.1 = bf16[2,1,256,768]{2,3,0,1:T(8,128)(2,1)S(1)} collective-permute-done((bf16[2,1,256,768]{2,3,0,1:T(8,128)(2,1)S(1)}, bf16[2,1,256,768]{2,3,0,1:T(8,128)(2,1)S(1)}, u32[]{:S(2)}, u32[]{:S(2)}) %collective-permute-start.1) | collective-permute-done | bytes 786464 | tf_op jit(solution)/shard_map/ppermute | solution.py:15
  41.7 0.1 select_bitcast_fusion
  41.8 0.1 pad_maximum_fusion
  41.9 2.8 %copy.39 = bf16[2,2,1,256,768]{3,1,2,0,4:T(2,128)(2,1)} copy(bf16[2,2,1,256,768]{3,4,1,2,0:T(8,128)(2,1)S(1)} %pad_maximum_fusion) | data formatting | bytes 3145728 | tf_op jit(solution)/shard_map/stack | solution.py:96
  44.7 0.0 copy-start.3
  44.7 15.5 %all-to-all-start = ((bf16[2,2,1,256,768]{3,1,2,0,4:T(2,128)(2,1)}), bf16[2,2,1,256,768]{3,1,2,0,4:T(2,128)(2,1)S(1)}, u32[]{:S(2)}, u32[]{:S(2)}) async-start(bf16[2,2,1,256,768]{3,1,2,0,4:T(2,128)(2,1)} %copy.39), calls=%async_computation | async-start | bytes 3145728 | tf_op jit(solution)/shard_map/all_to_all | solution.py:95
  60.2 0.0 copy-done.3
  60.2 0.7 fusion.53
  60.9 57.0 %all-to-all-done = bf16[2,2,1,256,768]{3,1,2,0,4:T(2,128)(2,1)S(1)} async-done(((bf16[2,2,1,256,768]{3,1,2,0,4:T(2,128)(2,1)}), bf16[2,2,1,256,768]{3,1,2,0,4:T(2,128)(2,1)S(1)}, u32[]{:S(2)}, u32[]{:S(2)}) %all-to-all-start) | async-done | bytes 1572896 | tf_op jit(solution)/shard_map/all_to_all | solution.py:95
  118.0 0.3 copy.48
  118.2 0.1 slice_bitcast_fusion.1
  118.4 4.5 %add_convert_fusion = bf16[2,24,256,32]{2,3,1,0:T(8,128)(2,1)} fusion(bf16[2,24,256,32]{2,3,1,0:T(8,128)(2,1)S(1)} %get-tuple-element.18, bf16[2,2,256,32]{2,3,1,0:T(8,128)(2,1)S(1)} %get-tuple-element.20, bf16[2,2,256,32]{2,3,1,0:T(8,128)(2,1)S(1)} %get-tuple-element.19, f32[]{:T(128)} %bitcast.40, f32[]{:T(128)} %bitcast.39, f32[]{:T(128)} %bitcast.38, ...), kind=kLoop, calls=%fused_computation.4 | loop fusion | flops 7471104 | bytes 1703956 | tf_op jit(solution)/shard_map/convert_element_type | solution.py:107
  (2 shorter events, 0.0 us)
Async XLA Ops:
  0.0 1.2 copy-start
  2.8 0.7 copy-start.4
  6.6 1.4 %copy-start.2 = (bf16[2,1,288,768]{3,2,1,0:T(8,128)(2,1)S(1)}, bf16[2,1,288,768]{3,2,1,0:T(8,128)(2,1)}, u32[]{:S(2)}) copy-start(bf16[2,1,288,768]{3,2,1,0:T(8,128)(2,1)} %param.6) | copy-start | bytes 2654212
  8.0 1.5 %copy-start.1 = (f32[288,2,768]{2,0,1:T(8,128)S(1)}, f32[288,2,768]{2,0,1:T(8,128)}, u32[]{:S(2)}) copy-start(f32[288,2,768]{2,0,1:T(8,128)} %fusion.20) | copy-start | bytes 5308420
  12.9 21.4 %collective-permute-start = (bf16[2,1,256,768]{2,3,0,1:T(8,128)(2,1)S(1)}, bf16[2,1,256,768]{2,3,0,1:T(8,128)(2,1)S(1)}, u32[]{:S(2)}, u32[]{:S(2)}) collective-permute-start(bf16[2,1,256,768]{2,3,0,1:T(8,128)(2,1)S(1)} %fusion), channel_id=1, source_target_pairs={{0,24},{24,48},{48,72},{72,96},{96,120},{120,144},{144,168},{168,1... | collective-permute-start | bytes 2359304 | tf_op jit(solution)/shard_map/ppermute | solution.py:14
  17.5 24.2 %collective-permute-start.1 = (bf16[2,1,256,768]{2,3,0,1:T(8,128)(2,1)S(1)}, bf16[2,1,256,768]{2,3,0,1:T(8,128)(2,1)S(1)}, u32[]{:S(2)}, u32[]{:S(2)}) collective-permute-start(bf16[2,1,256,768]{2,3,0,1:T(8,128)(2,1)S(1)} %fusion), channel_id=1, source_target_pairs={{24,0},{48,24},{72,48},{96,72},{120,96},{144,120},{168,144},{192,1... | collective-permute-start | bytes 2359304 | tf_op jit(solution)/shard_map/ppermute | solution.py:15
  44.7 15.5 %copy-start.3 = (f32[5]{0:T(128)S(1)}, f32[5]{0:T(128)}, u32[]{:S(2)}) copy-start(f32[5]{0:T(128)} %param.11) | copy-start | bytes 64
  44.7 73.2 %all-to-all-start = ((bf16[2,2,1,256,768]{3,1,2,0,4:T(2,128)(2,1)}), bf16[2,2,1,256,768]{3,1,2,0,4:T(2,128)(2,1)S(1)}, u32[]{:S(2)}, u32[]{:S(2)}) async-start(bf16[2,2,1,256,768]{3,1,2,0,4:T(2,128)(2,1)} %copy.39), calls=%async_computation | async-start | bytes 3145728 | tf_op jit(solution)/shard_map/all_to_all | solution.py:95
where the time goes:
time: 123 us
  waiting for transfers between devices  79.3 us (64%)
  starting transfers between devices  22 us (18%)
  local copies, waits for them, and re-layouts  9.48 us (8%)
  other arithmetic  8.18 us (7%)
  matrix products  3.73 us (3%)
    all_to_all x1, waiting for transfers between devices, body(): lax.all_to_all(jnp.stack([partial_value, borrowed]), 'freq', split_axis=4...  57 us
    all_to_all x1, starting transfers between devices, body(): lax.all_to_all(jnp.stack([partial_value, borrowed]), 'freq', split_axis=4...  15.5 us
    ppermute x1, waiting for transfers between devices, extended(): before = lax.ppermute(last, axis, up)  14.8 us
    ppermute x1, waiting for transfers between devices, extended(): after = lax.ppermute(leading, axis, down)  7.44 us
    ppermute x1, starting transfers between devices, extended(): before = lax.ppermute(last, axis, up)  4.61 us
    convert_element_type x1, other arithmetic, body(): return update.astype(jnp.bfloat16)  4.51 us
    broadcast_in_dim x2, local copies, waits for them, and re-layouts, body(): weight = jnp.repeat(flag_tiles.astype(jnp.float32), tile_width, axis=2)  2.87 us
    another operation x1, local copies, waits for them, and re-layouts, body(): jnp.stack([partial_value, borrowed])  2.77 us
  transfers between devices with their start and end apart: 3, of which 3 were waited for; matrix products, arithmetic and copies ran while one was open for 1% of the time, Pallas kernels for 0%

commit v1 on v0

--- a/solution.py
+++ b/solution.py
@@ -84,20 +84,8 @@
         antenna_sums / (1.0 + jnp.repeat(baseline_counts, tile_width, axis=2))[None]
     ).astype(jnp.bfloat16)
     half_width = (kernel.shape[0] - 1) // 2
-    beside = extended(partial_value, (("lst", 1),), 1)
-    position = lax.axis_index("freq")
-    groups = lax.axis_size("freq")
-    borrowed = jnp.where(
-        position >= groups - half_width,
-        beside[:, 0:1],
-        jnp.where(position < half_width, beside[:, 2:3], jnp.zeros_like(partial_value)),
-    )
-    received = lax.all_to_all(
-        jnp.stack([partial_value, borrowed]), "freq", split_axis=4, concat_axis=2, tiled=True
-    )
-    padded = jnp.concatenate(
-        [received[1][:, groups - half_width :], received[0], received[1][:, :half_width]], axis=1
-    )
+    received = lax.all_to_all(partial_value, "freq", split_axis=3, concat_axis=1, tiled=True)
+    padded = extended(received, (("lst", 1),), half_width)
     row_count = padded.shape[1] - 2 * half_width
     update = jnp.zeros((padded.shape[0], row_count, padded.shape[2], padded.shape[3]), jnp.float32)
     for shift_index in range(2 * half_width + 1):

time: 123 us -> 81.2 us (0.66)
  waiting for transfers between devices: 79.3 us -> 6.88 us
  blocking collectives: 0 us -> 48.2 us
  starting transfers between devices: 22 us -> 6.52 us
  local copies, waits for them, and re-layouts: 9.48 us -> 7.25 us
    all_to_all x1 -> x0, waiting for transfers between devices: 57 us -> none  [body(): lax.all_to_all(jnp.stack([partial_value, borrowed]), 'freq', split_axis=4...]
    all_to_all x0 -> x1, blocking collectives: none -> 48.2 us  [body(): lax.all_to_all(partial_value, 'freq', split_axis=3, concat_axis=1, tiled=...]
    all_to_all x1 -> x0, starting transfers between devices: 15.5 us -> none  [body(): lax.all_to_all(jnp.stack([partial_value, borrowed]), 'freq', split_axis=4...]
    ppermute x1, waiting for transfers between devices: 14.8 us -> 0.01 us  [extended(): before = lax.ppermute(last, axis, up)]
    another operation x1 -> x0, local copies, waits for them, and re-layouts: 2.77 us -> none  [body(): jnp.stack([partial_value, borrowed])]
  transfers between devices with their start and end apart: 3 -> 2, of which waited for: 3 -> 1; matrix products, arithmetic and copies ran while one was open for 1% -> 1% of each run, Pallas kernels for 0% -> 0%
where the time goes in v1:
time: 81.2 us; the launch traced here: 80.9 us
  blocking collectives  48.2 us (59%)
  other arithmetic  8.06 us (10%)
  local copies, waits for them, and re-layouts  7.25 us (9%)
  waiting for transfers between devices  6.88 us (8%)
  starting transfers between devices  6.52 us (8%)
  matrix products  3.75 us (5%)
    all_to_all x1, blocking collectives, body(): lax.all_to_all(partial_value, 'freq', split_axis=3, concat_axis=1, tiled=...  48.2 us
    ppermute x1, waiting for transfers between devices, extended(): after = lax.ppermute(leading, axis, down)  6.88 us
    convert_element_type x1, other arithmetic, body(): return update.astype(jnp.bfloat16)  4.62 us
    ppermute x1, starting transfers between devices, extended(): before = lax.ppermute(last, axis, up)  4.6 us
    broadcast_in_dim x2, local copies, waits for them, and re-layouts, body(): weight = jnp.repeat(flag_tiles.astype(jnp.float32), tile_width, axis=2)  2.87 us
    ppermute x1, starting transfers between devices, extended(): after = lax.ppermute(leading, axis, down)  1.92 us
    unnamed x10, local copies, waits for them, and re-layouts  1.77 us
    dot_general x1, matrix products, body(): jnp.einsum('ba,rtac->rtbc', hot_first, antenna_gains, preferred_element_t...  1.66 us
  transfers between devices with their start and end apart: 2, of which 1 were waited for; matrix products, arithmetic and copies ran while one was open for 1% of the time, Pallas kernels for 0%

profile of v1, /device:TPU:30, one launch (start us, length us, event | category | flops | bytes accessed | tf_op | source)
XLA Modules:
  0.0 80.9 jit_solution(16386883051123589949)
XLA Ops:
  0.0 0.0 copy-start
  0.0 0.8 slice_reduce_fusion.1
  0.8 0.4 copy-done
  1.2 1.7 %fusion.20 = f32[288,2,768]{2,0,1:T(8,128)} fusion(bf16[2,1,256,768]{3,2,1,0:T(8,128)(2,1)S(1)} %copy-done, s32[288]{0:T(512)S(1)} %get-tuple-element.5), kind=kOutput, calls=%fused_computation.43 | convolution fusion | flops 226566144 | bytes 2557056 | tf_op jit(solution)/shard_map/ba,rtac->rtbc/dot_general | solution.py:51
  2.8 0.0 copy-start.4
  2.8 0.4 convolution_bitcast_fusion
  3.3 0.3 copy-done.4
  3.5 0.1 copy.39
  3.7 1.4 %broadcast_in_dim.9 = f32[288,6,128]{2,1,0:T(8,128)} broadcast(f32[288,6]{1,0:T(8,128)S(1)} %bitcast.105), dimensions={0,1} | broadcast | bytes 891648 | tf_op jit(solution)/shard_map/broadcast_in_dim | solution.py:57
  5.1 1.5 %broadcast_in_dim.10 = f32[1,1,288,768]{3,2,1,0:T(8,128)S(1)} reshape(f32[288,6,128]{2,1,0:T(8,128)} %broadcast_in_dim.9) | data formatting | bytes 1769472 | tf_op jit(solution)/shard_map/broadcast_in_dim | solution.py:57
  6.6 0.0 copy-start.2
  6.6 1.4 %convert_element_type.52 = f32[2,1,288,768]{3,2,1,0:T(8,128)S(1)} convert(bf16[2,1,288,768]{3,2,1,0:T(8,128)(2,1)} %param.7) | non-fusion elementwise | flops 442368 | bytes 2654208 | tf_op jit(solution)/shard_map/convert_element_type | solution.py:62
  8.0 0.0 copy-done.2
  8.0 0.0 copy-start.1
  8.0 0.1 convert_element_type.51
  8.1 0.3 convolution_add_fusion
  8.4 1.1 %copy-done.1 = f32[288,2,768]{2,0,1:T(8,128)S(1)} copy-done((f32[288,2,768]{2,0,1:T(8,128)S(1)}, f32[288,2,768]{2,0,1:T(8,128)}, u32[]{:S(2)}) %copy-start.1) | copy-done | bytes 1769496
  9.5 0.2 fusion.14
  9.7 0.7 fusion.24
  10.4 0.5 fusion.22
  11.0 0.2 fusion.25
  11.2 0.2 fusion.23
  11.4 0.7 fusion.3
  12.1 0.1 broadcast_in_dim.11
  12.2 0.7 fusion
  12.9 0.8 %copy.37 = bf16[2,1,256,768]{2,0,1,3:T(2,128)(2,1)S(1)} copy(bf16[2,1,256,768]{2,3,0,1:T(8,128)(2,1)S(1)} %fusion) | data formatting | bytes 1572864 | tf_op jit(solution)/shard_map/convert_element_type | solution.py:85
  13.7 0.0 copy-start.3
  13.7 48.2 %all_to_all.18 = bf16[2,1,256,768]{2,0,1,3:T(2,128)(2,1)S(1)} all-to-all(bf16[2,1,256,768]{2,0,1,3:T(2,128)(2,1)S(1)} %copy.37), channel_id=1, replica_groups=mesh['lst'=32,'freq'=24] {'freq'}, dimensions={3} | all-to-all | bytes 1572864 | tf_op jit(solution)/shard_map/all_to_all | solution.py:87
  62.0 0.1 copy.46
  62.1 4.6 %collective-permute-start = (bf16[2,2,256,32]{2,3,1,0:T(8,128)(2,1)S(1)}, bf16[2,2,256,32]{2,3,1,0:T(8,128)(2,1)S(1)}, u32[]{:S(2)}, u32[]{:S(2)}) collective-permute-start(bf16[2,2,256,32]{2,3,1,0:T(8,128)(2,1)S(1)} %get-tuple-element.17), channel_id=1, source_target_pairs={{0,24},{24,48},{48,72},{72,96},{96,120},{120,144},{144,168},{168,1... | collective-permute-start | bytes 196616 | tf_op jit(solution)/shard_map/ppermute | solution.py:14
  66.8 1.9 %collective-permute-start.1 = (bf16[2,2,256,32]{2,3,1,0:T(8,128)(2,1)S(1)}, bf16[2,2,256,32]{2,3,1,0:T(8,128)(2,1)S(1)}, u32[]{:S(2)}, u32[]{:S(2)}) collective-permute-start(bf16[2,2,256,32]{2,3,1,0:T(8,128)(2,1)S(1)} %get-tuple-element.18), channel_id=1, source_target_pairs={{24,0},{48,24},{72,48},{96,72},{120,96},{144,120},{168,144},{192,1... | collective-permute-start | bytes 196616 | tf_op jit(solution)/shard_map/ppermute | solution.py:15
  68.7 0.0 copy-done.3
  68.7 0.7 fusion.53
  69.3 0.0 collective-permute-done
  69.3 6.9 %collective-permute-done.1 = bf16[2,2,256,32]{2,3,1,0:T(8,128)(2,1)S(1)} collective-permute-done((bf16[2,2,256,32]{2,3,1,0:T(8,128)(2,1)S(1)}, bf16[2,2,256,32]{2,3,1,0:T(8,128)(2,1)S(1)}, u32[]{:S(2)}, u32[]{:S(2)}) %collective-permute-start.1) | collective-permute-done | bytes 65568 | tf_op jit(solution)/shard_map/ppermute | solution.py:15
  76.2 4.6 %add_convert_fusion = bf16[2,24,256,32]{2,3,1,0:T(8,128)(2,1)} fusion(bf16[2,24,256,32]{2,3,1,0:T(8,128)(2,1)S(1)} %bitcast.102, bf16[2,2,256,32]{2,3,1,0:T(8,128)(2,1)S(1)} %collective-permute-done.1, bf16[2,2,256,32]{2,3,1,0:T(8,128)(2,1)S(1)} %collective-permute-done, f32[]{:T(128)} %bitcast.38, f32[]{:T(128)} %bitcast.37, f32[]{:T(128)} %bitcast.35, ...), kind=kLoop, calls=%fused_computation.2 | loop fusion | flops 7471104 | bytes 1703956 | tf_op jit(solution)/shard_map/convert_element_type | solution.py:95
  (2 shorter events, 0.0 us)
Async XLA Ops:
  0.0 1.2 %copy-start = (bf16[2,1,256,768]{3,2,1,0:T(8,128)(2,1)S(1)}, bf16[2,1,256,768]{3,2,1,0:T(8,128)(2,1)}, u32[]{:S(2)}) copy-start(bf16[2,1,256,768]{3,2,1,0:T(8,128)(2,1)} %param.8) | copy-start | bytes 2359300
  2.8 0.7 copy-start.4
  6.6 1.4 %copy-start.2 = (bf16[2,1,288,768]{3,2,1,0:T(8,128)(2,1)S(1)}, bf16[2,1,288,768]{3,2,1,0:T(8,128)(2,1)}, u32[]{:S(2)}) copy-start(bf16[2,1,288,768]{3,2,1,0:T(8,128)(2,1)} %param.6) | copy-start | bytes 2654212
  8.0 1.5 %copy-start.1 = (f32[288,2,768]{2,0,1:T(8,128)S(1)}, f32[288,2,768]{2,0,1:T(8,128)}, u32[]{:S(2)}) copy-start(f32[288,2,768]{2,0,1:T(8,128)} %fusion.20) | copy-start | bytes 5308420
  13.7 55.0 %copy-start.3 = (f32[5]{0:T(128)S(1)}, f32[5]{0:T(128)}, u32[]{:S(2)}) copy-start(f32[5]{0:T(128)} %param.11) | copy-start | bytes 64
  62.1 7.2 %collective-permute-start = (bf16[2,2,256,32]{2,3,1,0:T(8,128)(2,1)S(1)}, bf16[2,2,256,32]{2,3,1,0:T(8,128)(2,1)S(1)}, u32[]{:S(2)}, u32[]{:S(2)}) collective-permute-start(bf16[2,2,256,32]{2,3,1,0:T(8,128)(2,1)S(1)} %get-tuple-element.17), channel_id=1, source_target_pairs={{0,24},{24,48},{48,72},{72,96},{96,120},{120,144},{144,168},{168,1... | collective-permute-start | bytes 196616 | tf_op jit(solution)/shard_map/ppermute | solution.py:14
  66.8 9.5 %collective-permute-start.1 = (bf16[2,2,256,32]{2,3,1,0:T(8,128)(2,1)S(1)}, bf16[2,2,256,32]{2,3,1,0:T(8,128)(2,1)S(1)}, u32[]{:S(2)}, u32[]{:S(2)}) collective-permute-start(bf16[2,2,256,32]{2,3,1,0:T(8,128)(2,1)S(1)} %get-tuple-element.18), channel_id=1, source_target_pairs={{24,0},{48,24},{72,48},{96,72},{120,96},{144,120},{168,144},{192,1... | collective-permute-start | bytes 196616 | tf_op jit(solution)/shard_map/ppermute | solution.py:15

commit v2 on v1

v2 whole, which is shorter than its diff:
```python
import functools

import jax
import jax.numpy as jnp
from jax import lax
from jax.experimental import pallas as pl
from jax.experimental.pallas import tpu as pltpu
from jax.sharding import PartitionSpec as P

MESH = pl.DeviceIdType.MESH
LANES = 128
ROWS = 32
HALF = 2


def over_first(left, right):
    return lax.dot_general(
        left, right, (((0,), (0,)), ((), ())), preferred_element_type=jnp.float32
    )


def gradient_kernel(
    groups,
    blocks,
    vis_ref,
    model_ref,
    gain_ref,
    small_ref,
    kernel_ref,
    out_ref,
    data,
    model,
    gain,
    hot,
    inverse,
    weight,
    picked,
    terms,
    packed,
    bins,
    in_sem,
    send_sem,
    recv_sem,
    edge_send,
    edge_recv,
):
    tiles = data.shape[0]
    per_tile = groups // tiles
    width = LANES // per_tile
    count = data.shape[2]
    antennas = gain.shape[1]
    me = lax.axis_index("freq")
    block = lax.axis_index("lst")
    after = lax.rem(block + 1, blocks)
    before = lax.rem(block + blocks - 1, blocks)

    barrier = pltpu.get_barrier_semaphore()

    def greet(step, carry):
        peer = lax.rem(me + step, groups)
        pl.semaphore_signal(barrier, inc=1, device_id={"freq": peer}, device_id_type=MESH)
        return carry

    for peer in (before, after):
        pl.semaphore_signal(barrier, inc=1, device_id={"lst": peer}, device_id_type=MESH)
    lax.fori_loop(1, groups, greet, 0)

    def tile_of(i):
        turn = (1 - 2 * lax.rem(i, 2)) * ((i + 1) // 2)
        return lax.rem(me // per_tile + tiles // 2 + turn + tiles, tiles)

    def loads(i):
        lanes = pl.ds(pl.multiple_of(tile_of(i) * LANES, LANES), LANES)
        return [
            pltpu.make_async_copy(gain_ref.at[0, 0, :, lanes], gain.at[i, :, pl.ds(0, LANES)], in_sem.at[i, 0]),
            pltpu.make_async_copy(gain_ref.at[1, 0, :, lanes], gain.at[i, :, pl.ds(LANES, LANES)], in_sem.at[i, 1]),
            pltpu.make_async_copy(vis_ref.at[:, 0, :, lanes], data.at[i], in_sem.at[i, 2]),
            pltpu.make_async_copy(model_ref.at[:, 0, :, lanes], model.at[i], in_sem.at[i, 3]),
        ]

    def start_loads(i, carry):
        for copy in loads(i):
            copy.start()
        return carry

    lax.fori_loop(0, tiles, start_loads, 0)

    small = small_ref[...]
    row = lax.broadcasted_iota(jnp.int32, (small.shape[0], antennas), 0)
    antenna = lax.broadcasted_iota(jnp.int32, (count, antennas), 1).astype(jnp.float32)
    for which in range(2):
        label = over_first(small, (row == which).astype(jnp.bfloat16))
        hot[which * count : (which + 1) * count, :] = (label == antenna).astype(jnp.bfloat16)
    used = jnp.dot(
        small, hot[:count, :] + hot[count:, :], preferred_element_type=jnp.float32
    )
    inverse[...] = 1.0 / (1.0 + used)

    def compute(i):
        tile = tile_of(i)
        for copy in loads(i):
            copy.wait()
        picked[...] = jnp.dot(hot[...], gain[i], preferred_element_type=jnp.float32)
        weight[...] = over_first(small, (row[:, :LANES] == tile + 2).astype(jnp.bfloat16))
        for start in range(0, count, ROWS):
            here = slice(start, start + ROWS)
            there = slice(count + start, count + start + ROWS)
            first_re, first_im = picked[here, :LANES], picked[here, LANES:]
            second_re, second_im = picked[there, :LANES], picked[there, LANES:]
            data_re = data[i, 0, here, :].astype(jnp.float32)
            data_im = data[i, 1, here, :].astype(jnp.float32)
            model_re = model[i, 0, here, :].astype(jnp.float32)
            model_im = model[i, 1, here, :].astype(jnp.float32)
            flag = weight[here, :]
            cross_re = first_re * second_re + first_im * second_im
            cross_im = first_im * second_re - first_re * second_im
            pred_re = cross_re * model_re - cross_im * model_im
            pred_im = cross_re * model_im + cross_im * model_re
            resid_re = flag * (data_re - pred_re)
            resid_im = flag * (data_im - pred_im)
            along_re = second_re * model_re + second_im * model_im
            along_im = second_im * model_re - second_re * model_im
            terms[here, :LANES] = (resid_re * along_re - resid_im * along_im).astype(jnp.bfloat16)
            terms[here, LANES:] = (resid_re * along_im + resid_im * along_re).astype(jnp.bfloat16)
            other_re = first_re * model_re - first_im * model_im
            other_im = first_re * model_im + first_im * model_re
            terms[there, :LANES] = (resid_re * other_re + resid_im * other_im).astype(jnp.bfloat16)
            terms[there, LANES:] = (resid_re * other_im - resid_im * other_re).astype(jnp.bfloat16)
        sums = over_first(terms[...], hot[...])
        value = (sums * inverse[pl.ds(tile + 2, 1), :]).astype(jnp.bfloat16)
        for part in range(2):
            for j in range(per_tile):
                low = part * LANES + j * width
                packed[tile * per_tile + j, part] = value[low : low + width, :]

    def outgoing(peer):
        return pltpu.make_async_remote_copy(
            src_ref=packed.at[peer],
            dst_ref=bins.at[me + HALF],
            send_sem=send_sem.at[peer],
            recv_sem=recv_sem.at[me],
            device_id={"freq": peer},
            device_id_type=MESH,
        )

    def incoming(peer):
        return pltpu.make_async_remote_copy(
            src_ref=packed.at[peer],
            dst_ref=bins.at[peer + HALF],
            send_sem=send_sem.at[peer],
            recv_sem=recv_sem.at[peer],
            device_id={"freq": peer},
            device_id_type=MESH,
        )

    own = pltpu.make_async_copy(packed.at[me], bins.at[me + HALF], recv_sem.at[me])

    def send(i):
        tile = tile_of(i)
        for j in range(per_tile):
            peer = tile * per_tile + j

            @pl.when(peer != me)
            def _():
                outgoing(peer).start()

            @pl.when(peer == me)
            def _():
                own.start()

    def step(i, carry):
        compute(i)

        @pl.when(i == 1)
        def _():
            pl.semaphore_wait(barrier, groups + 1)

        @pl.when(i >= 1)
        def _():
            send(i - 1)

        return carry

    lax.fori_loop(0, tiles, step, 0)
    send(tiles - 1)

    def arrive(peer):
        @pl.when(peer != me)
        def _():
            incoming(peer).wait_recv()

        @pl.when(peer == me)
        def _():
            own.wait()

    def edge(which, source, target, device):
        return pltpu.make_async_remote_copy(
            src_ref=bins.at[pl.ds(source, HALF)],
            dst_ref=bins.at[pl.ds(target, HALF)],
            send_sem=edge_send.at[which],
            recv_sem=edge_recv.at[which],
            device_id={"lst": device},
            device_id_type=MESH,
        )

    to_before = edge(0, HALF, HALF + groups, before)
    to_after = edge(1, groups, 0, after)
    for peer in range(HALF):
        arrive(peer)
    to_before.start()
    for peer in range(groups - HALF, groups):
        arrive(peer)
    to_after.start()

    def arrive_loop(peer, carry):
        arrive(peer)
        return carry

    lax.fori_loop(HALF, groups - HALF, arrive_loop, 0)

    def smooth(t, carry=0):
        for part in range(2):
            total = kernel_ref[0] * bins[t, part].astype(jnp.float32)
            for shift in range(1, 2 * HALF + 1):
                total = total + kernel_ref[shift] * bins[t + shift, part].astype(jnp.float32)
            out_ref[part, t] = total.astype(jnp.bfloat16)
        return carry

    lax.fori_loop(HALF, groups - HALF, smooth, 0)
    to_before.wait_recv()
    to_after.wait_recv()
    for t in (*range(HALF), *range(groups - HALF, groups)):
        smooth(t)

    def sent(peer, carry):
        @pl.when(peer != me)
        def _():
            outgoing(peer).wait_send()

        return carry

    lax.fori_loop(0, groups, sent, 0)
    to_before.wait_send()
    to_after.wait_send()


def body(groups, blocks, visibilities, model_vis, antenna_gains, baseline_antenna_index, flag_tiles, kernel):
    count, channels = visibilities.shape[2:]
    antennas = antenna_gains.shape[2]
    tiles = channels // LANES
    width = channels // groups
    small = jnp.concatenate([baseline_antenna_index, flag_tiles[0].T]).astype(jnp.bfloat16)
    anywhere = pl.BlockSpec(memory_space=pl.ANY)
    smoothed = pl.pallas_call(
        functools.partial(gradient_kernel, groups, blocks),
        out_shape=jax.ShapeDtypeStruct((2, groups, width, antennas), jnp.bfloat16),
        in_specs=[
            anywhere,
            anywhere,
            anywhere,
            pl.BlockSpec(memory_space=pltpu.VMEM),
            pl.BlockSpec(memory_space=pltpu.SMEM),
        ],
        out_specs=pl.BlockSpec(memory_space=pltpu.VMEM),
        scratch_shapes=[
            pltpu.VMEM((tiles, 2, count, LANES), jnp.bfloat16),
            pltpu.VMEM((tiles, 2, count, LANES), jnp.bfloat16),
            pltpu.VMEM((tiles, antennas, 2 * LANES), jnp.bfloat16),
            pltpu.VMEM((2 * count, antennas), jnp.bfloat16),
            pltpu.VMEM((small.shape[0], antennas), jnp.float32),
            pltpu.VMEM((count, LANES), jnp.float32),
            pltpu.VMEM((2 * count, 2 * LANES), jnp.float32),
            pltpu.VMEM((2 * count, 2 * LANES), jnp.bfloat16),
            pltpu.VMEM((groups, 2, width, antennas), jnp.bfloat16),
            pltpu.VMEM((groups + 2 * HALF, 2, width, antennas), jnp.bfloat16),
            pltpu.SemaphoreType.DMA((tiles, 4)),
            pltpu.SemaphoreType.DMA((groups,)),
            pltpu.SemaphoreType.DMA((groups,)),
            pltpu.SemaphoreType.DMA((2,)),
            pltpu.SemaphoreType.DMA((2,)),
        ],
        compiler_params=pltpu.CompilerParams(collective_id=0, has_side_effects=True),
        name="gradient",
    )(visibilities, model_vis, antenna_gains, small, kernel)
    return jnp.swapaxes(smoothed, 2, 3)


def solution(mesh):
    in_specs = (
        P(None, ("lst", "freq"), None, None),
        P(None, ("lst", "freq"), None, None),
        P(None, ("lst", "freq"), None, None),
        P(),
        P(("lst", "freq"), None, None),
        P(),
    )
    out_specs = P(None, "lst", None, "freq")
    return jax.shard_map(
        functools.partial(body, mesh.shape["freq"], mesh.shape["lst"]),
        mesh=mesh,
        in_specs=in_specs,
        out_specs=out_specs,
        check_vma=False,
    )
```

time: 81.2 us -> 56.8 us (0.70)
  the two profiles are of different devices: /device:TPU:30 before, /device:TPU:1 now
where the time goes in v2:
time: 56.8 us; the launch traced here: 56.5 us
  Pallas kernels  52.5 us (92%)
  local copies, waits for them, and re-layouts  2.06 us (4%)
  other arithmetic  1.99 us (4%)
    pallas_call x1, Pallas kernels, body(): pl.pallas_call(functools.partial(gradient_kernel, groups, blocks), out_sh...  52.5 us
    unnamed x1, local copies, waits for them, and re-layouts  2.06 us

profile of v2, /device:TPU:1, one launch (start us, length us, event | category | flops | bytes accessed | tf_op | source)
XLA Modules:
  0.0 56.5 jit_solution(17204211334411824122)
XLA Ops:
  0.0 0.7 %convert.8 = bf16[2,288]{1,0:T(2,128)(2,1)S(1)} convert(s32[2,288]{1,0:T(2,128)} %param.9) | non-fusion elementwise | flops 576 | bytes 3456 | tf_op jit(solution)/shard_map/convert
  0.7 0.7 %fusion = bf16[6,288]{1,0:T(8,128)(2,1)S(1)} fusion(s32[1,288,6]{1,0,2:T(1,128)} %param.10), kind=kLoop, calls=%fused_computation.1 | loop fusion | flops 1728 | bytes 10368 | tf_op jit(solution)/shard_map/transpose | solution.py:252
  1.4 0.6 %pad_maximum_fusion.small_ref = bf16[8,288]{1,0:T(8,128)(2,1)} fusion(bf16[6,288]{1,0:T(8,128)(2,1)S(1)} %fusion, bf16[2,288]{1,0:T(2,128)(2,1)S(1)} %convert.8), kind=kLoop, calls=%fused_computation.2 | loop fusion | flops 9216 | bytes 9216 | tf_op jit(solution)/shard_map/concatenate | solution.py:252
  2.0 52.5 %gradient.1 = bf16[2,24,32,256]{3,2,1,0:T(8,128)(2,1)} custom-call(bf16[2,1,288,768]{3,2,1,0:T(8,128)(2,1)} %vis_ref.1, bf16[2,1,288,768]{3,2,1,0:T(8,128)(2,1)} %model_ref.1, bf16[2,1,256,768]{3,2,1,0:T(8,128)(2,1)} %gain_ref.1, bf16[8,288]{1,0:T(8,128)(2,1)} %pad_maximum_fusion.small_ref, f32[5]{0:T(128)} %kernel_ref.1), custom_call_target="tpu_custom_call" | custom-call | tf_op jit(solution)/shard_map/gradient/pallas_call | solution.py:254
  54.5 2.1 %copy.12 = bf16[2,24,256,32]{2,3,1,0:T(8,128)(2,1)} copy(bf16[2,24,256,32]{2,3,1,0:T(8,128)(2,1)} %bitcast.5) | data formatting | bytes 1572864

commit v3 on v2

--- a/solution.py
+++ b/solution.py
@@ -25,9 +25,9 @@
     vis_ref,
     model_ref,
     gain_ref,
-    small_ref,
-    kernel_ref,
-    out_ref,
+    index_ref,
+    flag_ref,
+    bins,
     data,
     model,
     gain,
@@ -37,7 +37,7 @@
     picked,
     terms,
     packed,
-    bins,
+    stack,
     in_sem,
     send_sem,
     recv_sem,
@@ -67,7 +67,8 @@
 
     def tile_of(i):
         turn = (1 - 2 * lax.rem(i, 2)) * ((i + 1) // 2)
-        return lax.rem(me // per_tile + tiles // 2 + turn + tiles, tiles)
+        first = jnp.where((me < HALF) | (me >= groups - HALF), 0, tiles // 2)
+        return lax.rem(me // per_tile + first + turn + tiles, tiles)
 
     def loads(i):
         lanes = pl.ds(pl.multiple_of(tile_of(i) * LANES, LANES), LANES)
@@ -85,7 +86,10 @@
 
     lax.fori_loop(0, tiles, start_loads, 0)
 
-    small = small_ref[...]
+    stack[0:2, :] = index_ref[...].astype(jnp.float32)
+    for k in range(tiles):
+        stack[k + 2 : k + 3, :] = flag_ref[k].astype(jnp.float32)
+    small = stack[...].astype(jnp.bfloat16)
     row = lax.broadcasted_iota(jnp.int32, (small.shape[0], antennas), 0)
     antenna = lax.broadcasted_iota(jnp.int32, (count, antennas), 1).astype(jnp.float32)
     for which in range(2):
@@ -193,24 +197,21 @@
         def _():
             own.wait()
 
-    def edge(which, source, target, device):
+    def edge(which):
+        forward = which < HALF
+        source = HALF + which if forward else groups + which - HALF
         return pltpu.make_async_remote_copy(
-            src_ref=bins.at[pl.ds(source, HALF)],
-            dst_ref=bins.at[pl.ds(target, HALF)],
+            src_ref=bins.at[source],
+            dst_ref=bins.at[source + groups if forward else source - groups],
             send_sem=edge_send.at[which],
             recv_sem=edge_recv.at[which],
-            device_id={"lst": device},
+            device_id={"lst": before if forward else after},
             device_id_type=MESH,
         )
 
-    to_before = edge(0, HALF, HALF + groups, before)
-    to_after = edge(1, groups, 0, after)
-    for peer in range(HALF):
-        arrive(peer)
-    to_before.start()
-    for peer in range(groups - HALF, groups):
-        arrive(peer)
-    to_after.start()
+    for which in range(2 * HALF):
+        arrive(which if which < HALF else groups + which - 2 * HALF)
+        edge(which).start()
 
     def arrive_loop(peer, carry):
         arrive(peer)
@@ -218,20 +219,8 @@
 
     lax.fori_loop(HALF, groups - HALF, arrive_loop, 0)
 
-    def smooth(t, carry=0):
-        for part in range(2):
-            total = kernel_ref[0] * bins[t, part].astype(jnp.float32)
-            for shift in range(1, 2 * HALF + 1):
-                total = total + kernel_ref[shift] * bins[t + shift, part].astype(jnp.float32)
-            out_ref[part, t] = total.astype(jnp.bfloat16)
-        return carry
-
-    lax.fori_loop(HALF, groups - HALF, smooth, 0)
-    to_before.wait_recv()
-    to_after.wait_recv()
-    for t in (*range(HALF), *range(groups - HALF, groups)):
-        smooth(t)
-
+    for which in range(2 * HALF):
+        edge(which).wait_recv()
     def sent(peer, carry):
         @pl.when(peer != me)
         def _():
@@ -240,8 +229,19 @@
         return carry
 
     lax.fori_loop(0, groups, sent, 0)
-    to_before.wait_send()
-    to_after.wait_send()
+    for which in range(2 * HALF):
+        edge(which).wait_send()
+
+
+def smooth_kernel(kernel_ref, bins_ref, out_ref):
+    def smooth(t, carry):
+        total = kernel_ref[0] * bins_ref[t, 0].astype(jnp.float32)
+        for shift in range(1, 2 * HALF + 1):
+            total = total + kernel_ref[shift] * bins_ref[t + shift, 0].astype(jnp.float32)
+        out_ref[0, t] = total.astype(jnp.bfloat16)
+        return carry
+
+    lax.fori_loop(0, out_ref.shape[1], smooth, 0)
 
 
 def body(groups, blocks, visibilities, model_vis, antenna_gains, baseline_antenna_index, flag_tiles, kernel):
@@ -249,39 +249,52 @@
     antennas = antenna_gains.shape[2]
     tiles = channels // LANES
     width = channels // groups
-    small = jnp.concatenate([baseline_antenna_index, flag_tiles[0].T]).astype(jnp.bfloat16)
+    rows = tiles + 2
+    held = groups + 2 * HALF
     anywhere = pl.BlockSpec(memory_space=pl.ANY)
-    smoothed = pl.pallas_call(
+    in_vmem = pl.BlockSpec(memory_space=pltpu.VMEM)
+    bins = pl.pallas_call(
         functools.partial(gradient_kernel, groups, blocks),
-        out_shape=jax.ShapeDtypeStruct((2, groups, width, antennas), jnp.bfloat16),
-        in_specs=[
-            anywhere,
-            anywhere,
-            anywhere,
-            pl.BlockSpec(memory_space=pltpu.VMEM),
-            pl.BlockSpec(memory_space=pltpu.SMEM),
-        ],
-        out_specs=pl.BlockSpec(memory_space=pltpu.VMEM),
+        out_shape=jax.ShapeDtypeStruct((held, 2, width, antennas), jnp.bfloat16),
+        in_specs=[anywhere, anywhere, anywhere, in_vmem, in_vmem],
+        out_specs=anywhere,
         scratch_shapes=[
             pltpu.VMEM((tiles, 2, count, LANES), jnp.bfloat16),
             pltpu.VMEM((tiles, 2, count, LANES), jnp.bfloat16),
             pltpu.VMEM((tiles, antennas, 2 * LANES), jnp.bfloat16),
             pltpu.VMEM((2 * count, antennas), jnp.bfloat16),
-            pltpu.VMEM((small.shape[0], antennas), jnp.float32),
+            pltpu.VMEM((rows, antennas), jnp.float32),
             pltpu.VMEM((count, LANES), jnp.float32),
             pltpu.VMEM((2 * count, 2 * LANES), jnp.float32),
             pltpu.VMEM((2 * count, 2 * LANES), jnp.bfloat16),
             pltpu.VMEM((groups, 2, width, antennas), jnp.bfloat16),
-            pltpu.VMEM((groups + 2 * HALF, 2, width, antennas), jnp.bfloat16),
+            pltpu.VMEM((rows, count), jnp.float32),
             pltpu.SemaphoreType.DMA((tiles, 4)),
             pltpu.SemaphoreType.DMA((groups,)),
             pltpu.SemaphoreType.DMA((groups,)),
-            pltpu.SemaphoreType.DMA((2,)),
-            pltpu.SemaphoreType.DMA((2,)),
+            pltpu.SemaphoreType.DMA((2 * HALF,)),
+            pltpu.SemaphoreType.DMA((2 * HALF,)),
         ],
         compiler_params=pltpu.CompilerParams(collective_id=0, has_side_effects=True),
         name="gradient",
-    )(visibilities, model_vis, antenna_gains, small, kernel)
+    )(
+        visibilities,
+        model_vis,
+        antenna_gains,
+        baseline_antenna_index,
+        jnp.transpose(flag_tiles, (2, 0, 1)),
+    )
+    smoothed = pl.pallas_call(
+        smooth_kernel,
+        out_shape=jax.ShapeDtypeStruct((2, groups, width, antennas), jnp.bfloat16),
+        grid=(2,),
+        in_specs=[
+            pl.BlockSpec(memory_space=pltpu.SMEM),
+            pl.BlockSpec((held, 1, width, antennas), lambda part: (0, part, 0, 0)),
+        ],
+        out_specs=pl.BlockSpec((1, groups, width, antennas), lambda part: (part, 0, 0, 0)),
+        name="smooth",
+    )(kernel, bins)
     return jnp.swapaxes(smoothed, 2, 3)
 
 

time: 56.8 us -> 51.4 us (0.905)
  the two profiles are of different devices: /device:TPU:1 before, /device:TPU:257 now
where the time goes in v3:
time: 51.4 us; the launch traced here: 51.2 us
  Pallas kernels  51.2 us (100%)
    pallas_call x1, Pallas kernels, body(): pl.pallas_call(functools.partial(gradient_kernel, groups, blocks), out_sh...  48.3 us
    pallas_call x1, Pallas kernels, body(): pl.pallas_call(smooth_kernel, out_shape=jax.ShapeDtypeStruct((2, groups,...  2.89 us

profile of v3, /device:TPU:257, one launch (start us, length us, event | category | flops | bytes accessed | tf_op | source)
XLA Modules:
  0.0 51.2 jit_solution(11107927487974767911)
XLA Ops:
  0.0 48.3 %gradient.1.bins_ref = bf16[28,2,32,256]{3,2,1,0:T(8,128)(2,1)} custom-call(bf16[2,1,288,768]{3,2,1,0:T(8,128)(2,1)} %vis_ref.1, bf16[2,1,288,768]{3,2,1,0:T(8,128)(2,1)} %model_ref.1, bf16[2,1,256,768]{3,2,1,0:T(8,128)(2,1)} %gain_ref.1, s32[2,288]{1,0:T(2,128)} %index_ref.1, s32[6,1,288]{2,1,0:T(1,128)} %bitcast.2), custom_call_target="tpu_custom_call" | custom-call | tf_op jit(solution)/shard_map/gradient/pallas_call | solution.py:256
  48.3 2.9 %smooth.1 = bf16[2,24,32,256]{3,2,1,0:T(8,128)(2,1)} custom-call(f32[5]{0:T(128)} %kernel_ref.1, bf16[28,2,32,256]{3,2,1,0:T(8,128)(2,1)} %gradient.1.bins_ref), custom_call_target="tpu_custom_call" | custom-call | tf_op jit(solution)/shard_map/smooth/pallas_call | solution.py:287

commit v4 on v3

--- a/solution.py
+++ b/solution.py
@@ -175,18 +175,14 @@
     def step(i, carry):
         compute(i)
 
-        @pl.when(i == 1)
+        @pl.when(i == 0)
         def _():
             pl.semaphore_wait(barrier, groups + 1)
 
-        @pl.when(i >= 1)
-        def _():
-            send(i - 1)
-
+        send(i)
         return carry
 
     lax.fori_loop(0, tiles, step, 0)
-    send(tiles - 1)
 
     def arrive(peer):
         @pl.when(peer != me)
@@ -233,15 +229,35 @@
         edge(which).wait_send()
 
 
-def smooth_kernel(kernel_ref, bins_ref, out_ref):
-    def smooth(t, carry):
-        total = kernel_ref[0] * bins_ref[t, 0].astype(jnp.float32)
-        for shift in range(1, 2 * HALF + 1):
-            total = total + kernel_ref[shift] * bins_ref[t + shift, 0].astype(jnp.float32)
-        out_ref[0, t] = total.astype(jnp.bfloat16)
-        return carry
-
-    lax.fori_loop(0, out_ref.shape[1], smooth, 0)
+def smooth_kernel(kernel_ref, bins_ref, out_ref, done, out_sem):
+    pieces, times, rows = done.shape[:3]
+    per_part = pieces // 2
+
+    def place(piece):
+        return piece // per_part, pl.ds(piece % per_part * rows, rows)
+
+    def store(piece):
+        part, here = place(piece)
+        return pltpu.make_async_copy(done.at[piece], out_ref.at[part, :, here], out_sem.at[piece])
+
+    taps = [kernel_ref[shift] for shift in range(2 * HALF + 1)]
+
+    def smooth(piece):
+        part, here = place(piece)
+        window = [bins_ref[t, part, here].astype(jnp.float32) for t in range(2 * HALF)]
+        for t in range(times):
+            window.append(bins_ref[t + 2 * HALF, part, here].astype(jnp.float32))
+            total = taps[0] * window[0]
+            for tap, value in zip(taps[1:], window[1:]):
+                total = total + tap * value
+            done[piece, t] = total.astype(jnp.bfloat16)
+            window.pop(0)
+
+    for piece in range(pieces):
+        smooth(piece)
+        store(piece).start()
+    for piece in range(pieces):
+        store(piece).wait()
 
 
 def body(groups, blocks, visibilities, model_vis, antenna_gains, baseline_antenna_index, flag_tiles, kernel):
@@ -255,9 +271,9 @@
     in_vmem = pl.BlockSpec(memory_space=pltpu.VMEM)
     bins = pl.pallas_call(
         functools.partial(gradient_kernel, groups, blocks),
-        out_shape=jax.ShapeDtypeStruct((held, 2, width, antennas), jnp.bfloat16),
+        out_shape=pltpu.VMEM((held, 2, width, antennas), jnp.bfloat16),
         in_specs=[anywhere, anywhere, anywhere, in_vmem, in_vmem],
-        out_specs=anywhere,
+        out_specs=in_vmem,
         scratch_shapes=[
             pltpu.VMEM((tiles, 2, count, LANES), jnp.bfloat16),
             pltpu.VMEM((tiles, 2, count, LANES), jnp.bfloat16),
@@ -284,15 +300,16 @@
         baseline_antenna_index,
         jnp.transpose(flag_tiles, (2, 0, 1)),
     )
+    bins = pltpu.with_memory_space_constraint(bins, pltpu.VMEM)
     smoothed = pl.pallas_call(
         smooth_kernel,
         out_shape=jax.ShapeDtypeStruct((2, groups, width, antennas), jnp.bfloat16),
-        grid=(2,),
-        in_specs=[
-            pl.BlockSpec(memory_space=pltpu.SMEM),
-            pl.BlockSpec((held, 1, width, antennas), lambda part: (0, part, 0, 0)),
+        in_specs=[pl.BlockSpec(memory_space=pltpu.SMEM), in_vmem],
+        out_specs=anywhere,
+        scratch_shapes=[
+            pltpu.VMEM((4, groups, width // 2, antennas), jnp.bfloat16),
+            pltpu.SemaphoreType.DMA((4,)),
         ],
-        out_specs=pl.BlockSpec((1, groups, width, antennas), lambda part: (part, 0, 0, 0)),
         name="smooth",
     )(kernel, bins)
     return jnp.swapaxes(smoothed, 2, 3)

time: 51.4 us -> 49.2 us (0.957)
  Pallas kernels: 51.2 us -> 49 us
    pallas_call x1, Pallas kernels: 48.3 us -> 47.1 us  [body(): pl.pallas_call(functools.partial(gradient_kernel, groups, blocks), out_sh...]
    pallas_call x1, Pallas kernels: 2.89 us -> 1.92 us  [body(): pl.pallas_call(smooth_kernel, out_shape=jax.ShapeDtypeStruct((2, groups,...]
where the time goes in v4:
time: 49.2 us; the launch traced here: 49 us
  Pallas kernels  49 us (100%)
    pallas_call x1, Pallas kernels, body(): pl.pallas_call(functools.partial(gradient_kernel, groups, blocks), out_sh...  47.1 us
    pallas_call x1, Pallas kernels, body(): pl.pallas_call(smooth_kernel, out_shape=jax.ShapeDtypeStruct((2, groups,...  1.92 us

profile of v4, /device:TPU:257, one launch (start us, length us, event | category | flops | bytes accessed | tf_op | source)
XLA Modules:
  0.0 49.0 jit_solution(13545247620742475122)
XLA Ops:
  0.0 47.1 %gradient.1.bins_ref = bf16[28,2,32,256]{3,2,1,0:T(8,128)(2,1)S(1)} custom-call(bf16[2,1,288,768]{3,2,1,0:T(8,128)(2,1)} %vis_ref.1, bf16[2,1,288,768]{3,2,1,0:T(8,128)(2,1)} %model_ref.1, bf16[2,1,256,768]{3,2,1,0:T(8,128)(2,1)} %gain_ref.1, s32[2,288]{1,0:T(2,128)} %index_ref.1, s32[6,1,288]{2,1,0:T(1,128)} %bitcast.2), custom_call_target="tpu_custom_call" | custom-call | tf_op jit(solution)/shard_map/gradient/pallas_call | solution.py:272
  47.1 1.9 %smooth.1 = bf16[2,24,32,256]{3,2,1,0:T(8,128)(2,1)} custom-call(f32[5]{0:T(128)} %kernel_ref.1, bf16[28,2,32,256]{3,2,1,0:T(8,128)(2,1)S(1)} %gradient.1.bins_ref), custom_call_target="tpu_custom_call" | custom-call | tf_op jit(solution)/shard_map/smooth/pallas_call | solution.py:304
